TPU v7x, 512 devices: a whole 4x8x8 slice. The times are simulated.
512 devices in a mesh: gx: 32 (over x, z), gy: 16 (over y, core).
Axes of the slice: x: 4, y: 8, z: 8, core: 2. Of those that a mesh axis runs over, the one named last changes fastest.
Arguments:
- right_side: float32 [2, 1024, 16384], P(None, 'gy', 'gx'), may hold values from -1.5 to 1.5
- faces: float32 [1024], P('gy'), may hold values from 0.149 to 6.69
- widths: float32 [1024], P('gy'), may hold values from 0.149 to 6.69
Outputs:
- pressure: float32 [2, 1024, 16384], P(None, 'gy', 'gx')
All inputs are finite; a program needn't handle non-finite values.
Results may differ from a plain program's by a relative error of at most 0.00045.
Values sent between devices are 32-bit elements; how exact they have to be, the bound alone decides.
A program may use at most 64 MiB of HBM per device.

v0:
```python
import math

import jax
import jax.numpy as jnp
from jax import lax
from jax.sharding import Mesh
from jax.sharding import PartitionSpec as P

RADIX = 128
GX = ("gx_0", "gx_1")
GX_GY = ("gx_0", "gx_1", "gy")


TWO_PI = 2.0 * math.pi
HIGHEST_PRECISION = lax.Precision.HIGHEST


def in_blocks(x, dim, length):
    before, after = (x.shape[:dim], x.shape[dim + 1 :])
    return jnp.moveaxis(x.reshape(*before, length, -1, *after), dim, 0)


def joined_along(parts, dim):
    shape = list(parts.shape[1:])
    shape[dim] *= parts.shape[0]
    return jnp.moveaxis(parts, 0, dim).reshape(shape)


def joined_exchange(x, axis, axes, splits, concats):
    sizes = [lax.axis_size(a) for a in axes]
    parts = in_blocks(x, splits[0], sizes[0])
    parts = jnp.moveaxis(in_blocks(parts, splits[1] + 1, sizes[1]), 0, 1)
    inside = parts.shape[2:]
    parts = parts.reshape(-1, *inside)
    parts = lax.all_to_all(parts, axis, split_axis=0, concat_axis=0, tiled=True)
    parts = joined_along(parts.reshape(*sizes, *inside), concats[0] + 1)
    return joined_along(parts, concats[1])


def gather_turned(arrays, axis, dims):
    turned = [jnp.moveaxis(a, dim, 0) for a, dim in zip(arrays, dims)]
    both = jnp.concatenate([t.reshape(len(t), -1) for t in turned], axis=1)
    result, at, done = (lax.all_gather(both, axis, axis=0, tiled=True), 0, [])
    for t, dim in zip(turned, dims):
        slab = result[:, at : at + t[0].size].reshape(-1, *t.shape[1:])
        done.append(jnp.moveaxis(slab, 0, dim))
        at += t[0].size
    return tuple(done)


def turned_blocks(parts, axes, order):
    inside = parts.shape[1:]
    result = parts.reshape(*(lax.axis_size(a) for a in axes), *inside)
    for k in order:
        result = lax.all_to_all(result, axes[k], k, k, tiled=True)
    return result.reshape(-1, *inside)


def one_axis_at_a_time(x, axes, order, split_dim, concat_dim):
    parts = in_blocks(x, split_dim, lax.axis_size(axes))
    return joined_along(turned_blocks(parts, axes, order), concat_dim)


def small_table(radix_size):
    indices = jnp.arange(radix_size, dtype=jnp.int32)
    phases = indices[:, None] * indices[None, :] % radix_size
    angles = phases.astype(jnp.float32) * (TWO_PI / radix_size)
    return (jnp.cos(angles), jnp.sin(angles))


def twiddle_table(radix_size):
    total_length = radix_size * radix_size
    indices = jnp.arange(radix_size, dtype=jnp.int32)
    phases = indices[:, None] * indices[None, :] % total_length
    angles = phases.astype(jnp.float32) * (TWO_PI / total_length)
    return (jnp.cos(angles), jnp.sin(angles))


def left_product(table, values):
    return jnp.einsum(
        "ab,...bc->...ac",
        table,
        values,
        precision=HIGHEST_PRECISION,
        preferred_element_type=jnp.float32,
    )


def right_product(values, table):
    return jnp.einsum(
        "...ab,bc->...ac",
        values,
        table,
        precision=HIGHEST_PRECISION,
        preferred_element_type=jnp.float32,
    )


def forward_dft(block_data):
    total_length = RADIX * RADIX
    lead_shape = block_data.shape[:1] + block_data.shape[2:-1]
    input_real = block_data[:, 0].reshape(lead_shape + (RADIX, RADIX))
    input_imag = block_data[:, 1].reshape(lead_shape + (RADIX, RADIX))
    cosine_small, sine_small = small_table(RADIX)
    cosine_turn, sine_turn = twiddle_table(RADIX)
    first_real = left_product(cosine_small, input_real) + left_product(sine_small, input_imag)
    first_imag = left_product(cosine_small, input_imag) - left_product(sine_small, input_real)
    turned_real = first_real * cosine_turn + first_imag * sine_turn
    turned_imag = first_imag * cosine_turn - first_real * sine_turn
    out_real = right_product(turned_real, cosine_small) + right_product(turned_imag, sine_small)
    out_imag = right_product(turned_imag, cosine_small) - right_product(turned_real, sine_small)
    return jnp.stack(
        [
            out_real.reshape(lead_shape + (total_length,)),
            out_imag.reshape(lead_shape + (total_length,)),
        ],
        axis=1,
    )


def inverse_dft(block_data):
    total_length = RADIX * RADIX
    lead_shape = block_data.shape[:1] + block_data.shape[2:-1]
    spec_real = block_data[:, 0].reshape(lead_shape + (RADIX, RADIX))
    spec_imag = block_data[:, 1].reshape(lead_shape + (RADIX, RADIX))
    cosine_small, sine_small = small_table(RADIX)
    cosine_turn, sine_turn = twiddle_table(RADIX)
    middle_real = right_product(spec_real, cosine_small) - right_product(spec_imag, sine_small)
    middle_imag = right_product(spec_imag, cosine_small) + right_product(spec_real, sine_small)
    turned_real = middle_real * cosine_turn - middle_imag * sine_turn
    turned_imag = middle_imag * cosine_turn + middle_real * sine_turn
    out_real = left_product(cosine_small, turned_real) - left_product(sine_small, turned_imag)
    out_imag = left_product(cosine_small, turned_imag) + left_product(sine_small, turned_real)
    scaling = 1.0 / total_length
    return jnp.stack(
        [
            (out_real * scaling).reshape(lead_shape + (total_length,)),
            (out_imag * scaling).reshape(lead_shape + (total_length,)),
        ],
        axis=1,
    )


def wave_terms(first_wave, wave_count, aspect_ratio):
    total_length = RADIX * RADIX
    positions = first_wave + jnp.arange(wave_count, dtype=jnp.int32)
    wave_index = positions // RADIX + RADIX * (positions % RADIX)
    kappa_term = 3.0 - 2.0 * jnp.cos(wave_index.astype(jnp.float32) * (TWO_PI / total_length))
    return kappa_term / float(aspect_ratio * aspect_ratio)


def build_rows(face_values, width_values, kappa_term):
    row_count = face_values.shape[0]
    wave_count = kappa_term.shape[0]
    positions = jnp.arange(row_count, dtype=jnp.int32)
    lower_row = jnp.where((positions == 0) & True, 0.0, -face_values)
    upper_face = jnp.concatenate([face_values[1:], jnp.zeros((1,), jnp.float32)])
    diagonal = (face_values + upper_face)[:, None] + width_values[:, None] * kappa_term[None, :]
    lower = jnp.broadcast_to(lower_row[:, None], (row_count, wave_count))
    upper = jnp.broadcast_to(-upper_face[:, None], (row_count, wave_count))
    return (lower, diagonal, upper)


def no_fetch(lower, diagonal, upper, source):
    return (
        jnp.zeros_like(lower),
        jnp.zeros_like(diagonal),
        jnp.zeros_like(upper),
        jnp.zeros_like(source),
    )


def split_rows(values, row_axis):
    half_rows = values.shape[row_axis] // 2
    shaped = values.reshape(values.shape[:row_axis] + (half_rows, 2) + values.shape[row_axis + 1 :])
    return (
        lax.index_in_dim(shaped, 0, row_axis + 1, False),
        lax.index_in_dim(shaped, 1, row_axis + 1, False),
    )


def reduce_levels(lower, diagonal, upper, source, fetch):
    stored = []
    depth_level = 0
    while lower.shape[0] > 1:
        lower_next, diag_next, upper_next, source_next = fetch(
            lower[:1], diagonal[:1], upper[:1], source[:, :, :1]
        )
        if depth_level == 0:
            upper = jnp.concatenate([upper[:-1], lower_next], axis=0)
            diagonal = jnp.concatenate([diagonal[:-1], diagonal[-1:]], axis=0)
        diag_next = jnp.where(True, 1.0, diag_next)
        lower_even, lower_odd = split_rows(lower, 0)
        diag_even, diag_odd = split_rows(diagonal, 0)
        upper_even, upper_odd = split_rows(upper, 0)
        source_even, source_odd = split_rows(source, 2)
        lower_right = jnp.concatenate([lower_even[1:], lower_next], axis=0)
        diag_right = jnp.concatenate([diag_even[1:], diag_next], axis=0)
        upper_right = jnp.concatenate([upper_even[1:], upper_next], axis=0)
        source_right = jnp.concatenate([source_even[:, :, 1:], source_next], axis=2)
        factor_left = -lower_odd / diag_even
        factor_right = -upper_odd / diag_right
        stored.append((lower_even, diag_even, upper_even, source_even))
        lower = factor_left * lower_even
        diagonal = diag_odd + factor_left * upper_even + factor_right * lower_right
        upper = factor_right * upper_right
        source = source_odd + factor_left * source_even + factor_right * source_right
        depth_level += 1
    return (stored, (lower, diagonal, upper, source))


def expand_levels(stored, top_values, previous):
    values = top_values
    for lower_even, diag_even, upper_even, source_even in reversed(stored):
        left_values = jnp.concatenate([previous, values[:, :, :-1]], axis=2)
        even_values = (source_even - lower_even * left_values - upper_even * values) / diag_even
        row_count = values.shape[2]
        values = jnp.stack([even_values, values], axis=3).reshape(
            values.shape[0], values.shape[1], 2 * row_count, values.shape[3]
        )
    return values


def local(right_side, faces, widths):
    levels, rows_local, columns = right_side.shape
    level_pairs = levels // 2
    groups = lax.axis_size(GX)
    row_groups = lax.axis_size("gy")
    total_length = RADIX * RADIX
    per_group = rows_local // groups
    aspect_ratio = 2 * rows_local
    line_rows = right_side.reshape(level_pairs, 2, groups, per_group, columns)
    spectrum = forward_dft(lax.all_to_all(line_rows, GX, split_axis=2, concat_axis=4, tiled=True))
    width_k = total_length // groups
    width_c = total_length // (groups * row_groups)
    moved_data = joined_exchange(spectrum, GX_GY, (GX, "gy"), (4, 4), (2, 2))
    planes = moved_data.reshape(level_pairs, 2, rows_local * row_groups, width_c)
    all_faces, all_widths = gather_turned((faces, widths), "gy", (0, 0))
    kappa_term = wave_terms(
        lax.axis_index(GX) * width_k + lax.axis_index("gy") * width_c, width_c, aspect_ratio
    )
    lower, diagonal, upper = build_rows(all_faces, all_widths, kappa_term)
    source = planes * (all_widths / aspect_ratio)[:, None]
    stored, final_row = reduce_levels(lower, diagonal, upper, source, no_fetch)
    empty_row = jnp.zeros((level_pairs, 2, 1, width_c), jnp.float32)
    solved = expand_levels(stored, final_row[3] / final_row[1], empty_row)
    returned = lax.all_to_all(
        solved.reshape(level_pairs, 2, row_groups * groups, per_group, width_c),
        "gy",
        split_axis=2,
        concat_axis=4,
        tiled=True,
    )
    real_lines = inverse_dft(lax.all_to_all(returned, GX, split_axis=2, concat_axis=4, tiled=True))
    final_blocks = one_axis_at_a_time(real_lines, GX, (0, 1), 4, 2)
    return final_blocks.reshape(levels, rows_local, columns)


def solution(mesh):
    finer = Mesh(mesh.devices.reshape(4, 8, mesh.shape["gy"]), ("gx_0", "gx_1", "gy"))
    in_specs = (P(None, "gy", GX), P("gy"), P("gy"))
    out_specs = P(None, "gy", GX)
    return jax.shard_map(local, mesh=finer, in_specs=in_specs, out_specs=out_specs, check_vma=False)
```

profile of v0, /device:TPU:1, one launch (start us, length us, event | category | flops | bytes accessed | tf_op | source)
XLA Modules:
  0.0 178.6 jit_solution(18133528471287255380)
XLA Ops:
  0.0 1.2 copy.662
  1.2 0.8 copy.663
  2.0 13.7 %all-to-all-start = ((f32[1,2,32,2,512]{4,3,1,0,2:T(2,128)}), f32[1,2,32,2,512]{4,3,1,0,2:T(2,128)S(1)}, u32[]{:S(2)}, u32[]{:S(2)}) async-start(f32[1,2,32,2,512]{4,3,1,0,2:T(2,128)} %copy.663), calls=%async_computation | async-start | bytes 524288 | tf_op jit(solution)/shard_map/all_to_all | solution.py:233
  16.4 18.4 %all-gather = f32[16,64,2]{1,2,0:T(2,128)S(1)} all-gather(f32[1,64,2]{1,2,0:T(2,128)S(1)} %maximum_bitcast_fusion.2), channel_id=1, replica_groups=mesh['gx_0'=4,'gx_1'=8,'gy'=16] {'gy'}, dimensions={0}, use_global_device_ids=true | all-gather | bytes 8704 | tf_op jit(solution)/shard_map/all_gather | solution.py:43
  39.4 1.1 fusion.162
  40.8 0.7 multiply_add_fusion.4
  41.6 0.8 fusion.165
  43.2 0.7 fusion.168
  55.0 0.7 broadcast_multiply_fusion.2
  60.3 0.8 copy.665
  61.2 1.9 %reshape.1317 = f32[512,1,128]{2,1,0:T(1,128)} reshape(f32[512,1,1,2,2,32]{5,4,3,2,1,0:T(2,128)S(1)} %bitcast.504) | data formatting | bytes 524288
  63.1 14.7 %all-to-all-start.1 = ((f32[512,1,128]{2,1,0:T(1,128)}), f32[512,1,128]{2,1,0:T(1,128)S(1)}, u32[]{:S(2)}, u32[]{:S(2)}) async-start(f32[512,1,128]{2,1,0:T(1,128)} %reshape.1317), calls=%async_computation.1 | async-start | bytes 524288 | tf_op jit(solution)/shard_map/all_to_all | solution.py:35
  78.3 0.7 copy.674
  80.7 13.8 %all-to-all-done.1 = f32[512,1,128]{2,1,0:T(1,128)S(1)} async-done(((f32[512,1,128]{2,1,0:T(1,128)}), f32[512,1,128]{2,1,0:T(1,128)S(1)}, u32[]{:S(2)}, u32[]{:S(2)}) %all-to-all-start.1) | async-done | bytes 262176 | tf_op jit(solution)/shard_map/all_to_all | solution.py:35
  95.1 1.3 reduce.26
  96.3 0.8 reshape.1318
  97.3 0.7 copy.667
  98.5 0.7 copy-done.11
  100.0 0.9 copy-done.4
  101.1 0.8 copy-done.13
  102.1 0.7 copy-done.6
  111.1 0.7 copy-done.2
  112.2 0.7 copy-done.3
  114.4 0.7 copy.748
  115.1 1.0 reshape.1319
  116.2 14.8 %all_to_all.69 = f32[16,1,4096]{2,1,0:T(1,128)S(1)} all-to-all(f32[16,1,4096]{2,1,0:T(1,128)S(1)} %reshape.1319), channel_id=1, replica_groups=mesh['gx_0'=4,'gx_1'=8,'gy'=16] {'gy'}, dimensions={0} | all-to-all | bytes 524288 | tf_op jit(solution)/shard_map/all_to_all | solution.py:247
  131.0 1.3 reduce.27
  132.3 0.9 reshape.1320
  134.4 15.3 %all_to_all.70 = f32[1,2,32,2,512]{4,3,1,0,2:T(2,128)S(1)} all-to-all(f32[1,2,32,2,512]{4,3,1,0,2:T(2,128)S(1)} %copy.751), channel_id=1, replica_groups=mesh['gx_0'=4,'gx_1'=8,'gy'=16] {'gx_0','gx_1'}, dimensions={2} | all-to-all | bytes 524288 | tf_op jit(solution)/shard_map/all_to_all | solution.py:254
  154.4 8.5 %all_to_all.71 = f32[4,8,1,2,1,2,512]{6,1,5,3,4,2,0:T(8,128)S(1)} all-to-all(f32[4,8,1,2,1,2,512]{6,1,5,3,4,2,0:T(8,128)S(1)} %copy.759), channel_id=1, replica_groups=mesh['gx_0'=4,'gx_1'=8,'gy'=16] {'gx_0'}, dimensions={0} | all-to-all | bytes 524288 | tf_op jit(solution)/shard_map/all_to_all | solution.py:55
  163.1 14.4 %all_to_all.72 = f32[4,8,1,2,1,2,512]{6,0,5,3,4,2,1:T(4,128)S(1)} all-to-all(f32[4,8,1,2,1,2,512]{6,0,5,3,4,2,1:T(4,128)S(1)} %copy.760), channel_id=1, replica_groups=mesh['gx_0'=4,'gx_1'=8,'gy'=16] {'gx_1'}, dimensions={1} | all-to-all | bytes 524288 | tf_op jit(solution)/shard_map/all_to_all | solution.py:55
  177.9 0.8 copy.763
  (346 shorter events, 41.9 us)
Async XLA Ops:
  2.0 53.8 %all-to-all-start = ((f32[1,2,32,2,512]{4,3,1,0,2:T(2,128)}), f32[1,2,32,2,512]{4,3,1,0,2:T(2,128)S(1)}, u32[]{:S(2)}, u32[]{:S(2)}) async-start(f32[1,2,32,2,512]{4,3,1,0,2:T(2,128)} %copy.663), calls=%async_computation | async-start | bytes 524288 | tf_op jit(solution)/shard_map/all_to_all | solution.py:233
  36.2 2.0 %copy-start.40 = (f32[512]{0:T(512)}, f32[512]{0:T(512)S(1)}, u32[]{:S(2)}) copy-start(f32[512]{0:T(512)S(1)} %get-tuple-element.7) | copy-start | bytes 6148
  36.2 2.4 %copy-start.42 = (f32[512]{0:T(512)}, f32[512]{0:T(512)S(1)}, u32[]{:S(2)}) copy-start(f32[512]{0:T(512)S(1)} %get-tuple-element.132) | copy-start | bytes 6148
  40.7 1.8 %copy-start.1 = (f32[128,1,32]{2,1,0:T(1,128)}, f32[128,1,32]{2,1,0:T(1,128)S(1)}, u32[]{:S(2)}) copy-start(f32[128,1,32]{2,1,0:T(1,128)S(1)} %get-tuple-element.74) | copy-start | bytes 49156
  42.5 1.5 copy-start.9
  44.0 1.4 copy-start.18
  45.3 1.3 copy-start.16
  45.4 1.9 %copy-start.28 = (f32[16,1,32]{2,1,0:T(1,128)}, f32[16,1,32]{2,1,0:T(1,128)S(1)}, u32[]{:S(2)}) copy-start(f32[16,1,32]{2,1,0:T(1,128)S(1)} %get-tuple-element.99) | copy-start | bytes 6148
  46.6 0.8 copy-start.22
  47.3 0.8 copy-start.37
  51.6 1.2 copy-start.53
  63.1 14.7 %copy-start.64 = (f32[2,1,32]{2,1,0:T(1,128)S(1)}, f32[2,1,32]{2,1,0:T(1,128)}, u32[]{:S(2)}) copy-start(f32[2,1,32]{2,1,0:T(1,128)} %get-tuple-element.119) | copy-start | bytes 772
  63.1 31.5 %all-to-all-start.1 = ((f32[512,1,128]{2,1,0:T(1,128)}), f32[512,1,128]{2,1,0:T(1,128)S(1)}, u32[]{:S(2)}, u32[]{:S(2)}) async-start(f32[512,1,128]{2,1,0:T(1,128)} %reshape.1317), calls=%async_computation.1 | async-start | bytes 524288 | tf_op jit(solution)/shard_map/all_to_all | solution.py:35
  77.8 1.3 copy-start
  98.4 0.8 copy-start.11
  99.9 0.9 copy-start.4
  101.1 0.8 copy-start.13
  102.1 0.8 copy-start.6
  102.1 0.8 copy-start.21
  102.9 0.7 copy-start.30
  103.7 2.2 %copy-start.61 = (f32[2,32]{1,0:T(2,128)S(1)}, f32[2,32]{1,0:T(2,128)}, u32[]{:S(2)}) copy-start(f32[2,32]{1,0:T(2,128)} %get-tuple-element.19) | copy-start | bytes 772
  104.4 2.8 %copy-start.54 = (f32[2,1,32]{2,1,0:T(1,128)S(1)}, f32[2,1,32]{2,1,0:T(1,128)}, u32[]{:S(2)}) copy-start(f32[2,1,32]{2,1,0:T(1,128)} %copy-done.53) | copy-start | bytes 772
  104.4 2.9 %copy-start.60 = (f32[2,1,32]{2,1,0:T(1,128)S(1)}, f32[2,1,32]{2,1,0:T(1,128)}, u32[]{:S(2)}) copy-start(f32[2,1,32]{2,1,0:T(1,128)} %get-tuple-element.118) | copy-start | bytes 772
  104.4 3.5 %copy-start.59 = (f32[4,1,32]{2,1,0:T(1,128)S(1)}, f32[4,1,32]{2,1,0:T(1,128)}, u32[]{:S(2)}) copy-start(f32[4,1,32]{2,1,0:T(1,128)} %get-tuple-element.109) | copy-start | bytes 1540
  109.3 0.8 copy-start.17
  109.3 0.8 copy-start.19
  110.1 0.8 copy-start.8
  110.2 0.8 copy-start.10
  110.2 0.8 copy-start.20
  111.0 0.8 copy-start.2
  111.0 0.9 copy-start.12
  111.9 0.9 copy-start.3
  (39 other events, 25.2 us)
where the time goes:
time: 180 us; the launch traced here: 179 us
  blocking collectives  71.4 us (40%)
  local copies, waits for them, and re-layouts  38.5 us (21%)
  starting transfers between devices  28.4 us (16%)
  other arithmetic  16.3 us (9%)
  waiting for transfers between devices  13.8 us (8%)
  matrix products  8.41 us (5%)
    unnamed x164, local copies, waits for them, and re-layouts  24.6 us
    all_to_all x2, blocking collectives, turned_blocks(): result = lax.all_to_all(result, axes[k], k, k, tiled=True)  22.9 us
    all_gather x1, blocking collectives, gather_turned(): result, at, done = (lax.all_gather(both, axis, axis=0, tiled=True), 0, [])  18.4 us
    all_to_all x1, blocking collectives, local(): lax.all_to_all(returned, GX, split_axis=2, concat_axis=4, tiled=True)  15.3 us
    all_to_all x1, blocking collectives, local(): lax.all_to_all(solved.reshape(level_pairs, 2, row_groups * groups, per_gr...  14.8 us
    all_to_all x1, starting transfers between devices, joined_exchange(): parts = lax.all_to_all(parts, axis, split_axis=0, concat_axis=0, tiled=True)  14.7 us
    all_to_all x1, waiting for transfers between devices, joined_exchange(): parts = lax.all_to_all(parts, axis, split_axis=0, concat_axis=0, tiled=True)  13.8 us
    all_to_all x1, starting transfers between devices, local(): lax.all_to_all(line_rows, GX, split_axis=2, concat_axis=4, tiled=True)  13.7 us
  transfers between devices with their start and end apart: 2, of which 1 were waited for; matrix products, arithmetic and copies ran while one was open for 10% of the time, Pallas kernels for 0%

commit v1 on v0

v1 whole, which is shorter than its diff:
```python
import functools

import jax
import jax.numpy as jnp
import numpy as np
from jax import lax
from jax.experimental import pallas as pl
from jax.experimental.pallas import tpu as pltpu
from jax.sharding import PartitionSpec as P

MESH = pl.DeviceIdType.MESH
RADIX = 128
NX = RADIX * RADIX
NZ = 8
GROUPS = 32
BLOCKS = 16
ROWS = 64
HALF = 32
ASPECT = 128
F32 = jnp.float32
BF16 = jnp.bfloat16
GROUNDED = 1e30


def split_table(table):
    table = np.asarray(table, np.float32)
    high = table.astype(BF16)
    low = (table - high.astype(np.float32)).astype(BF16)
    return high, low


def tables():
    small = 2.0 * np.pi * (np.outer(np.arange(RADIX), np.arange(RADIX)) % RADIX) / RADIX
    cosine, sine = np.cos(small), np.sin(small)
    turn = 2.0 * np.pi * np.outer(np.arange(RADIX), np.arange(RADIX)) / NX
    forward = np.zeros((GROUPS, 2, 4, GROUPS, 2, 4))
    cos6 = cosine.reshape(GROUPS, 4, GROUPS, 4)
    sin6 = sine.reshape(GROUPS, 4, GROUPS, 4)
    forward[:, 0, :, :, 0, :] = cos6
    forward[:, 0, :, :, 1, :] = sin6
    forward[:, 1, :, :, 0, :] = -sin6
    forward[:, 1, :, :, 1, :] = cos6
    forward = forward.reshape(256, 256)
    right = np.concatenate([cosine, sine], axis=1)
    turn_cos = np.zeros((GROUPS, 2, 4, RADIX))
    turn_sin = np.zeros((GROUPS, 2, 4, RADIX))
    turn_cos[:, 0] = np.cos(turn).reshape(GROUPS, 4, RADIX)
    turn_cos[:, 1] = turn_cos[:, 0]
    turn_sin[:, 0] = np.sin(turn).reshape(GROUPS, 4, RADIX)
    turn_sin[:, 1] = -turn_sin[:, 0]
    left = np.stack(split_table(forward) + split_table(forward.T / NX))
    sides = np.stack(split_table(right))
    turns = np.stack([turn_cos.reshape(256, RADIX), turn_sin.reshape(256, RADIX)]).astype(np.float32)
    return left, sides, turns


def split_values(values):
    high = values.astype(BF16)
    low = (values - high.astype(F32)).astype(BF16)
    return high, low


def dot(a, b):
    return jnp.dot(a, b, preferred_element_type=F32)


def swap_parts(values):
    shape = values.shape
    tiles = values.reshape(shape[0] // 8, 8, shape[1])
    return pltpu.roll(tiles, 4, 1).reshape(shape)


def kernel(x, faces, widths, left_hbm, sides_hbm, turns_hbm, out,
           s1, r1, s2, r2, s3, r3, s4, r4, left, sides, turns,
           coef, coefs, ends, ends_all, join, phi, psi, part_r, part_u, part_v, cur_i, cur_j,
           in_sem, tab_sem, send_sem, recv_sem, csend, crecv, esend, erecv, out_sem):
    g = lax.axis_index("gx")
    r = lax.axis_index("gy")

    def line_peer(i):
        return (g + i) % GROUPS

    def block_peer(i):
        return (r + i) % BLOCKS

    barrier = pltpu.get_barrier_semaphore()

    def greet_line(i, carry):
        pl.semaphore_signal(barrier, inc=1, device_id=(line_peer(i), r), device_id_type=MESH)
        return carry

    def greet_block(i, carry):
        pl.semaphore_signal(barrier, inc=1, device_id=(g, block_peer(i)), device_id_type=MESH)
        return carry

    lax.fori_loop(1, GROUPS, greet_line, 0)
    lax.fori_loop(1, BLOCKS, greet_block, 0)

    for h in range(2):
        for level in range(2):
            for c in range(4):
                pltpu.make_async_copy(
                    x.at[level, pl.ds(HALF * h, HALF), pl.ds(128 * c, 128)],
                    s1.at[h, :, level * 4 + c, :], in_sem.at[h]).start()
    pltpu.make_async_copy(left_hbm, left, tab_sem.at[0]).start()
    pltpu.make_async_copy(sides_hbm, sides, tab_sem.at[1]).start()
    pltpu.make_async_copy(turns_hbm, turns, tab_sem.at[2]).start()

    sub = lax.broadcasted_iota(jnp.int32, (8, 128), 0)
    lane = lax.broadcasted_iota(jnp.int32, (8, 128), 1)
    wave = 4 * g + sub % 4 + RADIX * lane
    kappa = (3.0 - 2.0 * jnp.cos(wave.astype(F32) * (2.0 * np.pi / NX))) / float(ASPECT * ASPECT)
    sign = jnp.where(sub < 4, 1.0, -1.0).astype(F32)

    def grow(i, abc):
        a, b, c = abc
        f = faces[i]
        inverse = 1.0 / (b + c + f)
        pass_b = b * inverse
        return a + pass_b * c, pass_b * f, widths[i] * kappa + (c * inverse) * f

    zero = jnp.zeros((8, 128), F32)
    a, b, c = lax.fori_loop(1, ROWS, grow, (zero, zero + faces[0], widths[0] * kappa))
    coef[0] = a
    coef[1] = b
    coef[2] = c

    pl.semaphore_wait(barrier, GROUPS - 1 + BLOCKS - 1)

    def exchange(source, target, h, at):
        def send(i, carry):
            q = line_peer(i)
            pltpu.make_async_remote_copy(
                source.at[h, q], target.at[h, g], send_sem.at[at], recv_sem.at[at],
                device_id=(q, r), device_id_type=MESH).start()
            return carry

        lax.fori_loop(1, GROUPS, send, 0)
        pltpu.make_async_copy(source.at[h, g], target.at[h, g], recv_sem.at[at]).start()

    def arrived(target, h, at):
        pltpu.make_async_copy(target.at[h], target.at[h], recv_sem.at[at]).wait()

    for h in range(2):
        pltpu.make_async_copy(s1.at[h], s1.at[h], in_sem.at[h]).wait()
        exchange(s1, r1, h, h)

    def send_coef(i, carry):
        pltpu.make_async_remote_copy(
            coef, coefs.at[r], csend, crecv,
            device_id=(g, block_peer(i)), device_id_type=MESH).start()
        return carry

    lax.fori_loop(1, BLOCKS, send_coef, 0)

    pltpu.make_async_copy(left_hbm, left, tab_sem.at[0]).wait()
    pltpu.make_async_copy(sides_hbm, sides, tab_sem.at[1]).wait()
    pltpu.make_async_copy(turns_hbm, turns, tab_sem.at[2]).wait()

    def left_product(at, values):
        high, low = split_values(values)
        return dot(left[at], high) + (dot(left[at], low) + dot(left[at + 1], high))

    def right_product(values, direction):
        high, low = split_values(values)
        both = dot(high, sides[0]) + (dot(low, sides[0]) + dot(high, sides[1]))
        tiles = swap_parts(both[:, 128:]).reshape(GROUPS, 8, 128)
        return both[:, :128].reshape(GROUPS, 8, 128) + tiles * (sign * direction)

    for h in range(2):
        arrived(r1, h, h)
        first = left_product(0, r1[h].reshape(256, 128))
        turned = first * turns[0] + swap_parts(first) * turns[1]
        s2[h] = right_product(turned, 1.0)
        exchange(s2, r2, h, 2 + h)

    pltpu.make_async_copy(coefs.at[pl.ds(0, BLOCKS - 1)], coefs.at[pl.ds(0, BLOCKS - 1)], crecv).wait()

    def from_below(m, shunt):
        a, b, c = coefs[m, 0], coefs[m, 1], coefs[m, 2]
        share = b / (b + (shunt + a))
        join[m] = share
        return c + (shunt + a) * share

    def from_above(i, shunt):
        m = BLOCKS - 1 - i
        a, b, c = coefs[m, 0], coefs[m, 1], coefs[m, 2]
        share = b / (b + (shunt + c))
        join[m] = share
        return a + (shunt + c) * share

    below = lax.fori_loop(0, r, from_below, zero + GROUNDED)
    above = lax.fori_loop(0, BLOCKS - 1 - r, from_above, zero)

    def up(i, state):
        shunt, through = state
        f = faces[i]
        share = f / (f + shunt)
        shunt = widths[i] * kappa + shunt * share
        through = through * share
        phi[i] = share
        part_r[i] = shunt
        part_u[i] = through
        return shunt, through

    lax.fori_loop(0, ROWS, up, (below, zero + 1.0))

    def down(j, state):
        shunt, through = state
        i = ROWS - 1 - j
        f = faces[i]
        total = 1.0 / (part_r[i] + shunt)
        part_r[i] = total
        part_u[i] = part_u[i] * total
        part_v[i] = through * total
        inner = widths[i] * kappa + shunt
        share = f / (f + inner)
        psi[i] = share
        return inner * share, through * share

    lax.fori_loop(0, ROWS, down, (above, zero + 1.0))

    for h in range(2):
        arrived(r2, h, 2 + h)

    def sweep(it, state):
        going_up, going_down = state
        for u in range(8):
            i = it * 8 + u
            going_up = r2[i // HALF, i % HALF] * (widths[i] * (1.0 / ASPECT)) + phi[i] * going_up
            cur_i[i] = going_up
            j = ROWS - 1 - i
            cur_j[j] = going_down
            going_down = psi[j] * (r2[j // HALF, j % HALF] * (widths[j] * (1.0 / ASPECT)) + going_down)
        return going_up, going_down

    going_up, going_down = lax.fori_loop(0, ROWS // 8, sweep, (zero, zero))
    ends[0] = going_up
    ends[1] = going_down

    def send_end(i, carry):
        q = block_peer(i)
        pltpu.make_async_remote_copy(
            ends.at[jnp.where(q < r, 1, 0)], ends_all.at[r], esend, erecv,
            device_id=(g, q), device_id_type=MESH).start()
        return carry

    lax.fori_loop(1, BLOCKS, send_end, 0)

    def own(it, carry):
        for u in range(8):
            i = it * 8 + u
            cur_i[i] = (cur_i[i] + cur_j[i]) * part_r[i]
        return carry

    lax.fori_loop(0, ROWS // 8, own, 0)

    pltpu.make_async_copy(ends_all.at[pl.ds(0, BLOCKS - 1)], ends_all.at[pl.ds(0, BLOCKS - 1)], erecv).wait()

    def add_below(m, current):
        return ends_all[m] + join[m] * current

    def add_above(i, current):
        m = BLOCKS - 1 - i
        return ends_all[m] + join[m] * current

    current_below = lax.fori_loop(0, r, add_below, zero)
    current_above = lax.fori_loop(0, BLOCKS - 1 - r, add_above, zero)

    for h in range(2):
        def finish(it, carry):
            for u in range(8):
                i = it * 8 + u
                m = HALF * h + i
                s3[h, i] = cur_i[m] + part_u[m] * current_below + part_v[m] * current_above
            return carry

        lax.fori_loop(0, HALF // 8, finish, 0)
        exchange(s3, r3, h, 4 + h)

    for h in range(2):
        arrived(r3, h, 4 + h)
        back = right_product(r3[h].reshape(256, 128), -1.0).reshape(256, 128)
        turned = back * turns[0] - swap_parts(back) * turns[1]
        s4[h] = left_product(2, turned).reshape(GROUPS, 8, 128)
        exchange(s4, r4, h, 6 + h)

    for h in range(2):
        arrived(r4, h, 6 + h)
        for level in range(2):
            for c in range(4):
                pltpu.make_async_copy(
                    r4.at[h, :, level * 4 + c, :],
                    out.at[level, pl.ds(HALF * h, HALF), pl.ds(128 * c, 128)], out_sem.at[h]).start()

    sent = (s1, s2, s3, s4)
    for n in range(4):
        for h in range(2):
            block = sent[n].at[h, pl.ds(0, GROUPS - 1)]
            pltpu.make_async_copy(block, block, send_sem.at[2 * n + h]).wait()
    pltpu.make_async_copy(coefs.at[pl.ds(0, BLOCKS - 1)], coefs.at[pl.ds(0, BLOCKS - 1)], csend).wait()
    pltpu.make_async_copy(ends_all.at[pl.ds(0, BLOCKS - 1)], ends_all.at[pl.ds(0, BLOCKS - 1)], esend).wait()
    for h in range(2):
        pltpu.make_async_copy(r4.at[h], r4.at[h], out_sem.at[h]).wait()


def local(right_side, faces, widths):
    left, sides, turns = tables()
    any_space = pl.BlockSpec(memory_space=pl.ANY)
    scalars = pl.BlockSpec(memory_space=pltpu.SMEM)
    moved = pltpu.VMEM((2, GROUPS, 8, 128), F32)
    rows = pltpu.VMEM((ROWS, 8, 128), F32)
    dma = pltpu.SemaphoreType.DMA
    return pl.pallas_call(
        kernel,
        out_shape=jax.ShapeDtypeStruct((2, ROWS, 512), F32),
        in_specs=[any_space, scalars, scalars, any_space, any_space, any_space],
        out_specs=any_space,
        scratch_shapes=[moved] * 8 + [
            pltpu.VMEM((4, 256, 256), BF16),
            pltpu.VMEM((2, 128, 256), BF16),
            pltpu.VMEM((2, 256, 128), F32),
            pltpu.VMEM((3, 8, 128), F32),
            pltpu.VMEM((BLOCKS, 3, 8, 128), F32),
            pltpu.VMEM((2, 8, 128), F32),
            pltpu.VMEM((BLOCKS, 8, 128), F32),
            pltpu.VMEM((BLOCKS, 8, 128), F32),
        ] + [rows] * 7 + [
            dma((2,)), dma((3,)), dma((8,)), dma((8,)), dma, dma, dma, dma, dma((2,)),
        ],
        compiler_params=pltpu.CompilerParams(collective_id=0, has_side_effects=True),
    )(right_side, faces, widths, left, sides, turns)


def solution(mesh):
    spec = P(None, "gy", "gx")
    return jax.shard_map(local, mesh=mesh, in_specs=(spec, P("gy"), P("gy")), out_specs=spec, check_vma=False)
```

time: 180 us -> 60.1 us (0.33)
  blocking collectives: 71.4 us -> 0 us
  Pallas kernels: 0 us -> 58.2 us
  local copies, waits for them, and re-layouts: 38.5 us -> 1.67 us
  starting transfers between devices: 28.4 us -> 0 us
  other arithmetic: 16.3 us -> 0 us
  waiting for transfers between devices: 13.8 us -> 0 us
  matrix products: 8.41 us -> 0 us
    pallas_call x0 -> x1, Pallas kernels: none -> 58.2 us  [local(): pl.pallas_call(kernel, out_shape=jax.ShapeDtypeStruct((2, ROWS, 512), F32...]
    all_to_all x4 -> x0, blocking collectives: 53 us -> none  [the longest x2 22.9 us: turned_blocks(): result = lax.all_to_all(result, axes[k], k, k, tiled=True)]
    all_to_all x2 -> x0, starting transfers between devices: 28.4 us -> none  [the longest x1 14.7 us: joined_exchange(): parts = lax.all_to_all(parts, axis, split_axis=0, concat_axis=0, tiled=True)]
    unnamed x164 -> x1, local copies, waits for them, and re-layouts: 24.6 us -> 1.67 us
    all_gather x1 -> x0, blocking collectives: 18.4 us -> none  [gather_turned(): result, at, done = (lax.all_gather(both, axis, axis=0, tiled=True), 0, [])]
    all_to_all x2 -> x0, waiting for transfers between devices: 13.8 us -> none  [the longest x1 13.8 us: joined_exchange(): parts = lax.all_to_all(parts, axis, split_axis=0, concat_axis=0, tiled=True)]
    dot_general x16 -> x0, matrix products: 8.41 us -> none  [the longest x8 4.31 us: left_product(): jnp.einsum('ab,...bc->...ac', table, values, precision=HIGHEST_PRECISION,...]
    add x18 -> x0, other arithmetic: 5.15 us -> none  [the longest x9 4.63 us: reduce_levels(): diagonal = diag_odd + factor_left * upper_even + factor_right * lower_right]
  transfers between devices with their start and end apart: 2 -> 0, of which waited for: 1 -> 0; matrix products, arithmetic and copies ran while one was open for 10% -> 0% of each run, Pallas kernels for 0% -> 0%
where the time goes in v1:
time: 60.1 us; the launch traced here: 59.9 us
  Pallas kernels  58.2 us (97%)
  local copies, waits for them, and re-layouts  1.67 us (3%)
    pallas_call x1, Pallas kernels, local(): pl.pallas_call(kernel, out_shape=jax.ShapeDtypeStruct((2, ROWS, 512), F32...  58.2 us
    unnamed x1, local copies, waits for them, and re-layouts  1.67 us

profile of v1, /device:TPU:1, one launch (start us, length us, event | category | flops | bytes accessed | tf_op | source)
XLA Modules:
  0.0 59.9 jit_solution(3359698171675230537)
XLA Ops:
  0.0 58.2 %shard_map.64 = f32[2,64,512]{2,1,0:T(8,128)} custom-call(f32[2,64,512]{2,1,0:T(8,128)} %x.1, f32[64]{0:T(128)} %faces.1, f32[64]{0:T(128)} %widths.1, bf16[4,256,256]{2,1,0:T(8,128)(2,1)} %constant.6.clone.left_hbm, bf16[2,128,256]{2,1,0:T(8,128)(2,1)} %constant.7.clone.sides_hbm, f32[2,256,128]{2,1,0:T(8,128)} %constant.8.clone.turns_hbm), custom_call_target="tpu_custom_call" | custom-call | tf_op jit(solution)/shard_map/pallas_call | solution.py:314
  58.2 1.7 %copy.8 = f32[2,64,512]{2,1,0:T(8,128)} copy(f32[2,64,512]{2,1,0:T(8,128)} %shard_map.64) | data formatting | bytes 524288

commit v2 on v1

--- a/solution.py
+++ b/solution.py
@@ -20,6 +20,16 @@
 F32 = jnp.float32
 BF16 = jnp.bfloat16
 GROUNDED = 1e30
+
+
+def ring_distance(step, size):
+    return min(step, size - step)
+
+
+LINE_STEPS = sorted(
+    [(dx, dz) for dx in range(4) for dz in range(NZ) if dx or dz],
+    key=lambda s: (-ring_distance(s[0], 4), -ring_distance(s[1], NZ)))
+BLOCK_STEPS = sorted(range(1, BLOCKS), key=lambda s: -ring_distance(s // 2, 8))
 
 
 def split_table(table):
@@ -70,32 +80,25 @@
     return pltpu.roll(tiles, 4, 1).reshape(shape)
 
 
-def kernel(x, faces, widths, left_hbm, sides_hbm, turns_hbm, out,
-           s1, r1, s2, r2, s3, r3, s4, r4, left, sides, turns,
-           coef, coefs, ends, ends_all, join, phi, psi, part_r, part_u, part_v, cur_i, cur_j,
-           in_sem, tab_sem, send_sem, recv_sem, csend, crecv, esend, erecv, out_sem):
+def kernel(x, faces_hbm, widths_hbm, left_hbm, sides_hbm, turns_hbm, r4,
+           s1, r1, s2, r2, s3, r3, s4, left, sides, turns, faces, widths,
+           coef, coefs, ends, ends_all, join, phi, psi, part_r, part_u, part_v, sum_up, sum_down, cur_i, cur_j,
+           in_sem, tab_sem, send_sem, recv_sem, csend, crecv, esend, erecv):
     g = lax.axis_index("gx")
     r = lax.axis_index("gy")
-
-    def line_peer(i):
-        return (g + i) % GROUPS
-
-    def block_peer(i):
-        return (r + i) % BLOCKS
+    along_x = [((g // NZ + d) % 4) * NZ for d in range(4)]
+    along_z = [(g % NZ + d) % NZ for d in range(NZ)]
+    line_peers = [along_x[dx] + along_z[dz] for dx, dz in LINE_STEPS]
+    block_peers = [(r // 2 * 2 + d // 2 * 2 + (r + d) % 2) % BLOCKS for d in BLOCK_STEPS]
 
     barrier = pltpu.get_barrier_semaphore()
-
-    def greet_line(i, carry):
-        pl.semaphore_signal(barrier, inc=1, device_id=(line_peer(i), r), device_id_type=MESH)
-        return carry
-
-    def greet_block(i, carry):
-        pl.semaphore_signal(barrier, inc=1, device_id=(g, block_peer(i)), device_id_type=MESH)
-        return carry
-
-    lax.fori_loop(1, GROUPS, greet_line, 0)
-    lax.fori_loop(1, BLOCKS, greet_block, 0)
-
+    for q in line_peers:
+        pl.semaphore_signal(barrier, inc=1, device_id=(q, r), device_id_type=MESH)
+    for q in block_peers:
+        pl.semaphore_signal(barrier, inc=1, device_id=(g, q), device_id_type=MESH)
+
+    pltpu.make_async_copy(faces_hbm, faces, tab_sem.at[3]).start()
+    pltpu.make_async_copy(widths_hbm, widths, tab_sem.at[4]).start()
     for h in range(2):
         for level in range(2):
             for c in range(4):
@@ -112,6 +115,9 @@
     kappa = (3.0 - 2.0 * jnp.cos(wave.astype(F32) * (2.0 * np.pi / NX))) / float(ASPECT * ASPECT)
     sign = jnp.where(sub < 4, 1.0, -1.0).astype(F32)
 
+    pltpu.make_async_copy(faces_hbm, faces, tab_sem.at[3]).wait()
+    pltpu.make_async_copy(widths_hbm, widths, tab_sem.at[4]).wait()
+
     def grow(i, abc):
         a, b, c = abc
         f = faces[i]
@@ -128,14 +134,10 @@
     pl.semaphore_wait(barrier, GROUPS - 1 + BLOCKS - 1)
 
     def exchange(source, target, h, at):
-        def send(i, carry):
-            q = line_peer(i)
+        for q in line_peers:
             pltpu.make_async_remote_copy(
                 source.at[h, q], target.at[h, g], send_sem.at[at], recv_sem.at[at],
                 device_id=(q, r), device_id_type=MESH).start()
-            return carry
-
-        lax.fori_loop(1, GROUPS, send, 0)
         pltpu.make_async_copy(source.at[h, g], target.at[h, g], recv_sem.at[at]).start()
 
     def arrived(target, h, at):
@@ -145,13 +147,10 @@
         pltpu.make_async_copy(s1.at[h], s1.at[h], in_sem.at[h]).wait()
         exchange(s1, r1, h, h)
 
-    def send_coef(i, carry):
+    for q in block_peers:
         pltpu.make_async_remote_copy(
             coef, coefs.at[r], csend, crecv,
-            device_id=(g, block_peer(i)), device_id_type=MESH).start()
-        return carry
-
-    lax.fori_loop(1, BLOCKS, send_coef, 0)
+            device_id=(g, q), device_id_type=MESH).start()
 
     pltpu.make_async_copy(left_hbm, left, tab_sem.at[0]).wait()
     pltpu.make_async_copy(sides_hbm, sides, tab_sem.at[1]).wait()
@@ -206,7 +205,7 @@
     lax.fori_loop(0, ROWS, up, (below, zero + 1.0))
 
     def down(j, state):
-        shunt, through = state
+        shunt, through, passed = state
         i = ROWS - 1 - j
         f = faces[i]
         total = 1.0 / (part_r[i] + shunt)
@@ -216,12 +215,33 @@
         inner = widths[i] * kappa + shunt
         share = f / (f + inner)
         psi[i] = share
-        return inner * share, through * share
-
-    lax.fori_loop(0, ROWS, down, (above, zero + 1.0))
-
+        sum_up[i] = passed * (widths[i] * (1.0 / ASPECT))
+        return inner * share, through * share, passed * phi[i]
+
+    lax.fori_loop(0, ROWS, down, (above, zero + 1.0, zero + 1.0))
+
+    def weigh(i, passed):
+        passed = passed * psi[i]
+        sum_down[i] = passed * (widths[i] * (1.0 / ASPECT))
+        return passed
+
+    lax.fori_loop(0, ROWS, weigh, zero + 1.0)
+
+    into_last = [zero] * 4
+    into_first = [zero] * 4
     for h in range(2):
         arrived(r2, h, 2 + h)
+        for i in range(HALF):
+            value = r2[h, i]
+            into_last[i % 4] = into_last[i % 4] + value * sum_up[HALF * h + i]
+            into_first[i % 4] = into_first[i % 4] + value * sum_down[HALF * h + i]
+    ends[0] = (into_last[0] + into_last[1]) + (into_last[2] + into_last[3])
+    ends[1] = (into_first[0] + into_first[1]) + (into_first[2] + into_first[3])
+
+    for q in block_peers:
+        pltpu.make_async_remote_copy(
+            ends.at[jnp.where(q < r, 1, 0)], ends_all.at[r], esend, erecv,
+            device_id=(g, q), device_id_type=MESH).start()
 
     def sweep(it, state):
         going_up, going_down = state
@@ -234,18 +254,7 @@
             going_down = psi[j] * (r2[j // HALF, j % HALF] * (widths[j] * (1.0 / ASPECT)) + going_down)
         return going_up, going_down
 
-    going_up, going_down = lax.fori_loop(0, ROWS // 8, sweep, (zero, zero))
-    ends[0] = going_up
-    ends[1] = going_down
-
-    def send_end(i, carry):
-        q = block_peer(i)
-        pltpu.make_async_remote_copy(
-            ends.at[jnp.where(q < r, 1, 0)], ends_all.at[r], esend, erecv,
-            device_id=(g, q), device_id_type=MESH).start()
-        return carry
-
-    lax.fori_loop(1, BLOCKS, send_end, 0)
+    lax.fori_loop(0, ROWS // 8, sweep, (zero, zero))
 
     def own(it, carry):
         for u in range(8):
@@ -287,11 +296,6 @@
 
     for h in range(2):
         arrived(r4, h, 6 + h)
-        for level in range(2):
-            for c in range(4):
-                pltpu.make_async_copy(
-                    r4.at[h, :, level * 4 + c, :],
-                    out.at[level, pl.ds(HALF * h, HALF), pl.ds(128 * c, 128)], out_sem.at[h]).start()
 
     sent = (s1, s2, s3, s4)
     for n in range(4):
@@ -300,36 +304,53 @@
             pltpu.make_async_copy(block, block, send_sem.at[2 * n + h]).wait()
     pltpu.make_async_copy(coefs.at[pl.ds(0, BLOCKS - 1)], coefs.at[pl.ds(0, BLOCKS - 1)], csend).wait()
     pltpu.make_async_copy(ends_all.at[pl.ds(0, BLOCKS - 1)], ends_all.at[pl.ds(0, BLOCKS - 1)], esend).wait()
-    for h in range(2):
-        pltpu.make_async_copy(r4.at[h], r4.at[h], out_sem.at[h]).wait()
+
+def unpack(r4, out, sem):
+    for h in range(2):
+        for level in range(2):
+            for c in range(4):
+                pltpu.make_async_copy(
+                    r4.at[h, :, level * 4 + c, :],
+                    out.at[level, pl.ds(HALF * h, HALF), pl.ds(128 * c, 128)], sem).start()
+    pltpu.make_async_copy(r4, r4, sem).wait()
 
 
 def local(right_side, faces, widths):
     left, sides, turns = tables()
     any_space = pl.BlockSpec(memory_space=pl.ANY)
-    scalars = pl.BlockSpec(memory_space=pltpu.SMEM)
     moved = pltpu.VMEM((2, GROUPS, 8, 128), F32)
     rows = pltpu.VMEM((ROWS, 8, 128), F32)
     dma = pltpu.SemaphoreType.DMA
-    return pl.pallas_call(
+    moved_back = pl.pallas_call(
         kernel,
-        out_shape=jax.ShapeDtypeStruct((2, ROWS, 512), F32),
-        in_specs=[any_space, scalars, scalars, any_space, any_space, any_space],
+        out_shape=jax.ShapeDtypeStruct((2, GROUPS, 8, 128), F32),
+        in_specs=[pl.BlockSpec(memory_space=pltpu.HBM)] * 6,
         out_specs=any_space,
-        scratch_shapes=[moved] * 8 + [
+        scratch_shapes=[moved] * 7 + [
             pltpu.VMEM((4, 256, 256), BF16),
             pltpu.VMEM((2, 128, 256), BF16),
             pltpu.VMEM((2, 256, 128), F32),
+            pltpu.SMEM((ROWS,), F32),
+            pltpu.SMEM((ROWS,), F32),
             pltpu.VMEM((3, 8, 128), F32),
             pltpu.VMEM((BLOCKS, 3, 8, 128), F32),
             pltpu.VMEM((2, 8, 128), F32),
             pltpu.VMEM((BLOCKS, 8, 128), F32),
             pltpu.VMEM((BLOCKS, 8, 128), F32),
-        ] + [rows] * 7 + [
-            dma((2,)), dma((3,)), dma((8,)), dma((8,)), dma, dma, dma, dma, dma((2,)),
+        ] + [rows] * 9 + [
+            dma((2,)), dma((5,)), dma((8,)), dma((8,)), dma, dma, dma, dma,
         ],
-        compiler_params=pltpu.CompilerParams(collective_id=0, has_side_effects=True),
-    )(right_side, faces, widths, left, sides, turns)
+        compiler_params=pltpu.CompilerParams(
+            collective_id=0, has_side_effects=True, vmem_limit_bytes=12 * 1024 * 1024),
+    )(*[pltpu.with_memory_space_constraint(a, pltpu.HBM) for a in (right_side, faces, widths, left, sides, turns)])
+    return pl.pallas_call(
+        unpack,
+        out_shape=jax.ShapeDtypeStruct((2, ROWS, 512), F32),
+        in_specs=[any_space],
+        out_specs=any_space,
+        scratch_shapes=[dma],
+        compiler_params=pltpu.CompilerParams(vmem_limit_bytes=1024 * 1024),
+    )(moved_back)
 
 
 def solution(mesh):

time: 60.1 us -> 53.9 us (0.90)
  Pallas kernels: 58.2 us -> 53.8 us
  local copies, waits for them, and re-layouts: 1.67 us -> 0 us
    pallas_call x1 -> x2, Pallas kernels: 58.2 us -> 53.8 us  [the longest x1 53.1 us: local(): pl.pallas_call(kernel, out_shape=jax.ShapeDtypeStruct((2, GROUPS, 8, 128)...]
    unnamed x1 -> x0, local copies, waits for them, and re-layouts: 1.67 us -> none
where the time goes in v2:
time: 53.9 us; the launch traced here: 53.8 us
  Pallas kernels  53.8 us (100%)
    pallas_call x1, Pallas kernels, local(): pl.pallas_call(kernel, out_shape=jax.ShapeDtypeStruct((2, GROUPS, 8, 128)...  53.1 us

profile of v2, /device:TPU:1, one launch (start us, length us, event | category | flops | bytes accessed | tf_op | source)
XLA Modules:
  0.0 53.8 jit_solution(14398595237961320473)
XLA Ops:
  0.0 53.1 %shard_map.64.r4 = f32[2,32,8,128]{3,2,1,0:T(8,128)S(1)} custom-call(f32[2,64,512]{2,1,0:T(8,128)} %x.1, f32[64]{0:T(128)} %faces_hbm.1, f32[64]{0:T(128)} %widths_hbm.1, bf16[4,256,256]{2,1,0:T(8,128)(2,1)} %constant.6.clone.left_hbm, bf16[2,128,256]{2,1,0:T(8,128)(2,1)} %constant.7.clone.sides_hbm, f32[2,256,128]{2,1,0:T(8,128)} %constant.8.clone.turns_hbm), custom_call_target="tpu_custom_call" | custom-call | tf_op jit(solution)/shard_map/pallas_call | solution.py:324
  53.1 0.7 %shard_map.65 = f32[2,64,512]{2,1,0:T(8,128)} custom-call(f32[2,32,8,128]{3,2,1,0:T(8,128)S(1)} %shard_map.64.r4), custom_call_target="tpu_custom_call" | custom-call | tf_op jit(solution)/shard_map/pallas_call | solution.py:346

commit v3 on v2

--- a/solution.py
+++ b/solution.py
@@ -28,7 +28,7 @@
 
 LINE_STEPS = sorted(
     [(dx, dz) for dx in range(4) for dz in range(NZ) if dx or dz],
-    key=lambda s: (-ring_distance(s[0], 4), -ring_distance(s[1], NZ)))
+    key=lambda s: -(1.9 * ring_distance(s[0], 4) + ring_distance(s[1], NZ)))
 BLOCK_STEPS = sorted(range(1, BLOCKS), key=lambda s: -ring_distance(s // 2, 8))
 
 
@@ -58,8 +58,13 @@
     turn_cos[:, 1] = turn_cos[:, 0]
     turn_sin[:, 0] = np.sin(turn).reshape(GROUPS, 4, RADIX)
     turn_sin[:, 1] = -turn_sin[:, 0]
-    left = np.stack(split_table(forward) + split_table(forward.T / NX))
-    sides = np.stack(split_table(right))
+    left = []
+    for table in (forward, forward.T / NX):
+        high, low = split_table(table)
+        left.append(np.concatenate([high, high, low], axis=1))
+    left = np.stack(left)
+    high, low = split_table(right)
+    sides = np.concatenate([high, high, low], axis=0)
     turns = np.stack([turn_cos.reshape(256, RADIX), turn_sin.reshape(256, RADIX)]).astype(np.float32)
     return left, sides, turns
 
@@ -80,22 +85,33 @@
     return pltpu.roll(tiles, 4, 1).reshape(shape)
 
 
-def kernel(x, faces_hbm, widths_hbm, left_hbm, sides_hbm, turns_hbm, r4,
-           s1, r1, s2, r2, s3, r3, s4, left, sides, turns, faces, widths,
-           coef, coefs, ends, ends_all, join, phi, psi, part_r, part_u, part_v, sum_up, sum_down, cur_i, cur_j,
+def kernel(x, faces_hbm, widths_hbm, left_hbm, sides_hbm, turns_hbm, out,
+           s1, r1, s2, r2, s3, r3, s4, r4, left, sides, turns, faces, widths,
+           coef, coefs, ends, ends_all, join, gain_below, gain_above, phi, psi, part_r, part_u, part_v, sum_up, sum_down, cur_i, cur_j,
            in_sem, tab_sem, send_sem, recv_sem, csend, crecv, esend, erecv):
     g = lax.axis_index("gx")
     r = lax.axis_index("gy")
+    barrier = pltpu.get_barrier_semaphore()
+
+    def farthest_first(i, size):
+        return (size // 2 + (i + 1) // 2 * (1 - 2 * (i % 2))) % size
+
+    def greet_line(i, carry):
+        q = (g // NZ + farthest_first(i // NZ, 4)) % 4 * NZ + (g % NZ + farthest_first(i % NZ, NZ)) % NZ
+        pl.semaphore_signal(barrier, inc=1, device_id=(q, r), device_id_type=MESH)
+        return carry
+
+    def greet_block(i, carry):
+        pl.semaphore_signal(barrier, inc=1, device_id=(g, (r + i) % BLOCKS), device_id_type=MESH)
+        return carry
+
+    lax.fori_loop(0, GROUPS - 1, greet_line, 0)
+    lax.fori_loop(1, BLOCKS, greet_block, 0)
+
     along_x = [((g // NZ + d) % 4) * NZ for d in range(4)]
     along_z = [(g % NZ + d) % NZ for d in range(NZ)]
     line_peers = [along_x[dx] + along_z[dz] for dx, dz in LINE_STEPS]
     block_peers = [(r // 2 * 2 + d // 2 * 2 + (r + d) % 2) % BLOCKS for d in BLOCK_STEPS]
-
-    barrier = pltpu.get_barrier_semaphore()
-    for q in line_peers:
-        pl.semaphore_signal(barrier, inc=1, device_id=(q, r), device_id_type=MESH)
-    for q in block_peers:
-        pl.semaphore_signal(barrier, inc=1, device_id=(g, q), device_id_type=MESH)
 
     pltpu.make_async_copy(faces_hbm, faces, tab_sem.at[3]).start()
     pltpu.make_async_copy(widths_hbm, widths, tab_sem.at[4]).start()
@@ -158,11 +174,11 @@
 
     def left_product(at, values):
         high, low = split_values(values)
-        return dot(left[at], high) + (dot(left[at], low) + dot(left[at + 1], high))
+        return dot(left[at], jnp.concatenate([high, low, high], axis=0))
 
     def right_product(values, direction):
         high, low = split_values(values)
-        both = dot(high, sides[0]) + (dot(low, sides[0]) + dot(high, sides[1]))
+        both = dot(jnp.concatenate([high, low, high], axis=1), sides[...])
         tiles = swap_parts(both[:, 128:]).reshape(GROUPS, 8, 128)
         return both[:, :128].reshape(GROUPS, 8, 128) + tiles * (sign * direction)
 
@@ -190,6 +206,24 @@
 
     below = lax.fori_loop(0, r, from_below, zero + GROUNDED)
     above = lax.fori_loop(0, BLOCKS - 1 - r, from_above, zero)
+
+    for m in range(BLOCKS):
+        gain_below[m] = zero
+        gain_above[m] = zero
+    ends_all[r] = zero
+
+    def reach_below(i, gain):
+        m = r - 1 - i
+        gain_below[m] = gain
+        return gain * join[m]
+
+    def reach_above(i, gain):
+        m = r + 1 + i
+        gain_above[m] = gain
+        return gain * join[m]
+
+    lax.fori_loop(0, r, reach_below, zero + 1.0)
+    lax.fori_loop(0, BLOCKS - 1 - r, reach_above, zero + 1.0)
 
     def up(i, state):
         shunt, through = state
@@ -266,15 +300,14 @@
 
     pltpu.make_async_copy(ends_all.at[pl.ds(0, BLOCKS - 1)], ends_all.at[pl.ds(0, BLOCKS - 1)], erecv).wait()
 
-    def add_below(m, current):
-        return ends_all[m] + join[m] * current
-
-    def add_above(i, current):
-        m = BLOCKS - 1 - i
-        return ends_all[m] + join[m] * current
-
-    current_below = lax.fori_loop(0, r, add_below, zero)
-    current_above = lax.fori_loop(0, BLOCKS - 1 - r, add_above, zero)
+    def total(gains):
+        terms = [ends_all[m] * gains[m] for m in range(BLOCKS)]
+        while len(terms) > 1:
+            terms = [terms[m] + terms[m + 1] for m in range(0, len(terms), 2)]
+        return terms[0]
+
+    current_below = total(gain_below)
+    current_above = total(gain_above)
 
     for h in range(2):
         def finish(it, carry):
@@ -291,11 +324,15 @@
         arrived(r3, h, 4 + h)
         back = right_product(r3[h].reshape(256, 128), -1.0).reshape(256, 128)
         turned = back * turns[0] - swap_parts(back) * turns[1]
-        s4[h] = left_product(2, turned).reshape(GROUPS, 8, 128)
+        s4[h] = left_product(1, turned).reshape(GROUPS, 8, 128)
         exchange(s4, r4, h, 6 + h)
 
     for h in range(2):
         arrived(r4, h, 6 + h)
+        for level in range(2):
+            for c in range(4):
+                for t in range(0, HALF, 8):
+                    out[level, pl.ds(HALF * h + t, 8), pl.ds(128 * c, 128)] = r4[h, pl.ds(t, 8), level * 4 + c, :]
 
     sent = (s1, s2, s3, s4)
     for n in range(4):
@@ -305,14 +342,11 @@
     pltpu.make_async_copy(coefs.at[pl.ds(0, BLOCKS - 1)], coefs.at[pl.ds(0, BLOCKS - 1)], csend).wait()
     pltpu.make_async_copy(ends_all.at[pl.ds(0, BLOCKS - 1)], ends_all.at[pl.ds(0, BLOCKS - 1)], esend).wait()
 
-def unpack(r4, out, sem):
-    for h in range(2):
-        for level in range(2):
-            for c in range(4):
-                pltpu.make_async_copy(
-                    r4.at[h, :, level * 4 + c, :],
-                    out.at[level, pl.ds(HALF * h, HALF), pl.ds(128 * c, 128)], sem).start()
-    pltpu.make_async_copy(r4, r4, sem).wait()
+def place(held, out, sem):
+    for level in range(2):
+        for t in range(0, ROWS, 16):
+            pltpu.make_async_copy(held.at[level, pl.ds(t, 16)], out.at[level, pl.ds(t, 16)], sem).start()
+    pltpu.make_async_copy(held, out, sem).wait()
 
 
 def local(right_side, faces, widths):
@@ -321,20 +355,22 @@
     moved = pltpu.VMEM((2, GROUPS, 8, 128), F32)
     rows = pltpu.VMEM((ROWS, 8, 128), F32)
     dma = pltpu.SemaphoreType.DMA
-    moved_back = pl.pallas_call(
+    held = pl.pallas_call(
         kernel,
-        out_shape=jax.ShapeDtypeStruct((2, GROUPS, 8, 128), F32),
+        out_shape=jax.ShapeDtypeStruct((2, ROWS, 512), F32),
         in_specs=[pl.BlockSpec(memory_space=pltpu.HBM)] * 6,
-        out_specs=any_space,
-        scratch_shapes=[moved] * 7 + [
-            pltpu.VMEM((4, 256, 256), BF16),
-            pltpu.VMEM((2, 128, 256), BF16),
+        out_specs=pl.BlockSpec(memory_space=pltpu.VMEM),
+        scratch_shapes=[moved] * 8 + [
+            pltpu.VMEM((2, 256, 768), BF16),
+            pltpu.VMEM((384, 256), BF16),
             pltpu.VMEM((2, 256, 128), F32),
             pltpu.SMEM((ROWS,), F32),
             pltpu.SMEM((ROWS,), F32),
             pltpu.VMEM((3, 8, 128), F32),
             pltpu.VMEM((BLOCKS, 3, 8, 128), F32),
             pltpu.VMEM((2, 8, 128), F32),
+            pltpu.VMEM((BLOCKS, 8, 128), F32),
+            pltpu.VMEM((BLOCKS, 8, 128), F32),
             pltpu.VMEM((BLOCKS, 8, 128), F32),
             pltpu.VMEM((BLOCKS, 8, 128), F32),
         ] + [rows] * 9 + [
@@ -344,13 +380,13 @@
             collective_id=0, has_side_effects=True, vmem_limit_bytes=12 * 1024 * 1024),
     )(*[pltpu.with_memory_space_constraint(a, pltpu.HBM) for a in (right_side, faces, widths, left, sides, turns)])
     return pl.pallas_call(
-        unpack,
+        place,
         out_shape=jax.ShapeDtypeStruct((2, ROWS, 512), F32),
         in_specs=[any_space],
         out_specs=any_space,
         scratch_shapes=[dma],
         compiler_params=pltpu.CompilerParams(vmem_limit_bytes=1024 * 1024),
-    )(moved_back)
+    )(held)
 
 
 def solution(mesh):

time: 53.9 us -> 53.6 us (level)
  no operation moved by 1% of the time
where the time goes in v3:
time: 53.6 us; the launch traced here: 53.5 us
  Pallas kernels  53.5 us (100%)
    pallas_call x1, Pallas kernels, local(): pl.pallas_call(kernel, out_shape=jax.ShapeDtypeStruct((2, ROWS, 512), F32...  52.8 us

profile of v3, /device:TPU:1, one launch (start us, length us, event | category | flops | bytes accessed | tf_op | source)
XLA Modules:
  0.0 53.5 jit_solution(770136940768314453)
XLA Ops:
  0.0 52.8 %shard_map.64.held = f32[2,64,512]{2,1,0:T(8,128)S(1)} custom-call(f32[2,64,512]{2,1,0:T(8,128)} %x.1, f32[64]{0:T(128)} %faces_hbm.1, f32[64]{0:T(128)} %widths_hbm.1, bf16[2,256,768]{2,1,0:T(8,128)(2,1)} %constant.6.clone.left_hbm, bf16[384,256]{1,0:T(8,128)(2,1)} %constant.7.clone.sides_hbm, f32[2,256,128]{2,1,0:T(8,128)} %constant.8.clone.turns_hbm), custom_call_target="tpu_custom_call" | custom-call | tf_op jit(solution)/shard_map/pallas_call | solution.py:358
  52.8 0.7 %shard_map.65 = f32[2,64,512]{2,1,0:T(8,128)} custom-call(f32[2,64,512]{2,1,0:T(8,128)S(1)} %shard_map.64.held), custom_call_target="tpu_custom_call" | custom-call | tf_op jit(solution)/shard_map/pallas_call | solution.py:382

commit v4 on v3

--- a/solution.py
+++ b/solution.py
@@ -150,7 +150,7 @@
     pl.semaphore_wait(barrier, GROUPS - 1 + BLOCKS - 1)
 
     def exchange(source, target, h, at):
-        for q in line_peers:
+        for q in (line_peers[::-1] if at in (2, 6) else line_peers):
             pltpu.make_async_remote_copy(
                 source.at[h, q], target.at[h, g], send_sem.at[at], recv_sem.at[at],
                 device_id=(q, r), device_id_type=MESH).start()

time: 53.6 us -> 53.5 us (level)
  no operation moved by 1% of the time
where the time goes in v4:
time: 53.5 us; the launch traced here: 53.3 us
  Pallas kernels  53.3 us (100%)
    pallas_call x1, Pallas kernels, local(): pl.pallas_call(kernel, out_shape=jax.ShapeDtypeStruct((2, ROWS, 512), F32...  52.6 us

profile of v4, /device:TPU:1, one launch (start us, length us, event | category | flops | bytes accessed | tf_op | source)
XLA Modules:
  0.0 53.3 jit_solution(6965469337175170448)
XLA Ops:
  0.0 52.6 %shard_map.64.held = f32[2,64,512]{2,1,0:T(8,128)S(1)} custom-call(f32[2,64,512]{2,1,0:T(8,128)} %x.1, f32[64]{0:T(128)} %faces_hbm.1, f32[64]{0:T(128)} %widths_hbm.1, bf16[2,256,768]{2,1,0:T(8,128)(2,1)} %constant.6.clone.left_hbm, bf16[384,256]{1,0:T(8,128)(2,1)} %constant.7.clone.sides_hbm, f32[2,256,128]{2,1,0:T(8,128)} %constant.8.clone.turns_hbm), custom_call_target="tpu_custom_call" | custom-call | tf_op jit(solution)/shard_map/pallas_call | solution.py:358
  52.6 0.7 %shard_map.65 = f32[2,64,512]{2,1,0:T(8,128)} custom-call(f32[2,64,512]{2,1,0:T(8,128)S(1)} %shard_map.64.held), custom_call_target="tpu_custom_call" | custom-call | tf_op jit(solution)/shard_map/pallas_call | solution.py:382
